TPU v7x, 32 devices: a whole 2x2x4 slice. The times are simulated.
32 devices in a mesh: groups: 2 (over y), tok: 4 (over z), mod: 2 (over x), fsdp: 2 (over core).
Axes of the slice: x: 2, y: 2, z: 4, core: 2. Of those that a mesh axis runs over, the one named last changes fastest.
Arguments:
- residual: bfloat16 [1024, 4096], P(('groups', 'tok'), ('fsdp', 'mod')), parts along dimension 0, may hold values from -30 to 30
- context: bfloat16 [1024, 4096], P(('groups', 'tok'), ('mod', 'fsdp')), parts along dimension 0, may hold values from -6 to 6
- out_proj: bfloat16 [4096, 4096], P('tok', ('fsdp', 'mod')), may hold values from -0.09375 to 0.09375
- norm_gain: bfloat16 [2, 4096], P(None, ('fsdp', 'mod')), may hold values from 0.099609375 to 1.8984375
- router_weight: bfloat16 [4096, 4], P(('fsdp', 'mod')), may hold values from -0.25 to 0.25
- block_modality: int32 [8], P(('groups', 'tok')), parts along dimension 0, may hold values from 0 to 1, as said below
- expert_rows: int32 [4, 128], P(None, ('groups', 'tok')), parts along dimension 1, may hold values from -1 to 127, as said below
- gate_weight: bfloat16 [4, 4096, 11008], P('mod', 'fsdp', 'tok'), may hold values from -0.09375 to 0.09375
- up_weight: bfloat16 [4, 4096, 11008], P('mod', 'fsdp', 'tok'), may hold values from -0.09375 to 0.09375
- down_weight: bfloat16 [4, 11008, 4096], P('mod', 'tok', 'fsdp'), may hold values from -0.0546875 to 0.0546875
Outputs:
- expert_out: bfloat16 [1024, 4096], P(('groups', 'tok'), ('fsdp', 'mod')), parts along dimension 0
There are 2 independent parts, one for each index of `groups`. A program takes and returns all parts, laid end to end along the dimension named above; an argument that names none is the same for every part. Nothing has to cross between parts.
Inputs may be any that keep to these rules, and one draw needn't show every extreme that they name: `block_modality`: both modalities occur in every window. `expert_rows`: slot s = t * 16 + j of expert e names a row among tokens t * 128 to (t + 1) * 128 - 1, or is -1 if unused. Experts below 2 take only text tokens, the others only image tokens; no expert takes a token twice; in each aligned block of 16 slots the used ones come first; every expert fills all 16 slots of at least one index of tok whose tokens have the expert's modality.
All inputs are finite; a program needn't handle non-finite values.
Results may differ from a plain program's by a relative error of at most 0.02.
Values may be sent and summed in bfloat16 or wider, within the bound.
No kernel may reach another device: no remote copies, remote signals or barrier semaphores. Data moves between devices by JAX's collectives and lax.ppermute only.
A program may use at most 192 MiB of HBM per device.

v0:
```python
import jax
import jax.numpy as jnp
from jax import lax
from jax.sharding import PartitionSpec as P

D = 4096
BLOCK = 128


def local(
    residual,
    context,
    out_proj,
    norm_gain,
    router_weight,
    block_modality,
    expert_rows,
    gate_weight,
    up_weight,
    down_weight,
):
    full_context = lax.all_gather(context, ("mod", "fsdp"), axis=1, tiled=True)
    token_count = residual.shape[0]
    projected = jnp.dot(
        full_context,
        lax.all_gather(out_proj, "tok", axis=0, tiled=True),
        preferred_element_type=jnp.float32,
    )
    hidden = residual.astype(jnp.float32) + projected
    token_mod = jnp.repeat(block_modality, BLOCK)
    gain_table = norm_gain.astype(jnp.float32)
    token_gain = jnp.where(token_mod[:, None] == 0, gain_table[0][None, :], gain_table[1][None, :])
    gained = hidden * token_gain
    router_table = router_weight.astype(jnp.float32)
    squares = jnp.sum(hidden * hidden, axis=1)
    square_total = lax.psum(squares, ("mod", "fsdp"))
    inverse = lax.rsqrt(square_total / D + 1e-05)
    normed = gained * inverse[:, None]
    logits = lax.psum(
        jnp.dot(normed, router_table, precision=lax.Precision.HIGHEST), ("mod", "fsdp")
    )
    score = jax.nn.sigmoid(logits)
    normed_rows = normed.astype(jnp.bfloat16)
    local_experts = gate_weight.shape[0]
    first_expert = lax.axis_index("mod") * local_experts
    row_ids = lax.iota(jnp.int32, token_count)
    own_rows = lax.dynamic_slice_in_dim(expert_rows, first_expert, local_experts, 0)
    own_pick = (own_rows[:, :, None] == row_ids[None, None, :]).astype(jnp.bfloat16)
    half_rows = lax.all_gather(normed_rows, "mod", axis=1, tiled=True)
    chosen = jnp.einsum(
        "ecr,rd->ecd", own_pick, half_rows, preferred_element_type=jnp.float32
    ).astype(jnp.bfloat16)
    unit_count = gate_weight.shape[2]
    piece = lax.all_gather(chosen, "tok", axis=1, tiled=True)
    gate_part = jnp.einsum("esd,edf->esf", piece, gate_weight, preferred_element_type=jnp.float32)
    up_part = jnp.einsum("esd,edf->esf", piece, up_weight, preferred_element_type=jnp.float32)
    partial_in = jnp.concatenate((gate_part, up_part), axis=2)
    summed_in = lax.psum(partial_in.astype(jnp.bfloat16), "fsdp").astype(jnp.float32)
    activation = (jax.nn.silu(summed_in[:, :, :unit_count]) * summed_in[:, :, unit_count:]).astype(
        jnp.bfloat16
    )
    expert_value = lax.psum_scatter(
        jnp.einsum(
            "esf,efd->sed", activation, down_weight, preferred_element_type=jnp.float32
        ).astype(jnp.bfloat16),
        "tok",
        scatter_dimension=0,
        tiled=True,
    ).astype(jnp.float32)
    own_score = lax.dynamic_slice_in_dim(score, first_expert, local_experts, 1)
    pick_table = own_pick.astype(jnp.float32)
    slot_score = jnp.einsum("ecr,re->ce", pick_table, own_score, precision=lax.Precision.HIGHEST)
    scaled = expert_value * slot_score[:, :, None]
    mixed_rows = jnp.einsum("ecr,ced->rd", pick_table, scaled, precision=lax.Precision.HIGHEST)
    combined = lax.psum_scatter(
        mixed_rows.astype(jnp.bfloat16), "mod", scatter_dimension=1, tiled=True
    )
    return combined


def solution(mesh):
    placed = (
        P(("groups", "tok"), ("fsdp", "mod")),
        P(("groups", "tok"), ("mod", "fsdp")),
        P("tok", ("fsdp", "mod")),
        P(None, ("fsdp", "mod")),
        P(("fsdp", "mod"), None),
        P(("groups", "tok")),
        P(None, ("groups", "tok")),
        P("mod", "fsdp", "tok"),
        P("mod", "fsdp", "tok"),
        P("mod", "tok", "fsdp"),
    )
    return jax.shard_map(
        local,
        mesh=mesh,
        in_specs=placed,
        out_specs=P(("groups", "tok"), ("fsdp", "mod")),
        check_vma=False,
    )
```

profile of v0, /device:TPU:0, one launch (start us, length us, event | category | flops | bytes accessed | tf_op | source)
XLA Modules:
  0.0 316.3 jit_solution(1377281258367514044)
XLA Ops:
  6.5 0.0 copy-start
  6.5 0.0 all-gather.3.cloned.1.call-start
  6.5 0.7 all-gather.3.cloned.1.call-update
  7.3 0.0 all-gather.5.cloned.1.call-start
  7.3 0.7 all-gather.5.cloned.1.call-update
  8.0 0.0 all-reduce.2.cloned.1.call-start
  8.7 0.7 convert_element_type.35
  9.4 0.7 constant_dynamic-slice_fusion.1
  10.1 18.3 %all-gather.3.cloned.1.call-done = bf16[128,4096]{1,0:T(8,128)(2,1)} async-done(((bf16[128,1024]{1,0:T(8,128)(2,1)}), bf16[128,4096]{1,0:T(8,128)(2,1)}) %all-gather.3.cloned.1.call-update) | async-done | bytes 1048592 | tf_op jit(solution)/shard_map/all_gather | solution.py:22
  28.4 151.2 %all-gather.5.cloned.1.call-done = bf16[4096,1024]{1,0:T(8,128)(2,1)} async-done(((bf16[1024,1024]{1,0:T(8,128)(2,1)}), bf16[4096,1024]{1,0:T(8,128)(2,1)}) %all-gather.5.cloned.1.call-update) | async-done | bytes 8388624 | tf_op jit(solution)/shard_map/all_gather | solution.py:26
  179.6 5.0 %multiply_reduce_fusion = (f32[128]{0:T(128)S(1)}, f32[128,1024]{1,0:T(8,128)S(1)}) fusion(bf16[128,4096]{1,0:T(8,128)(2,1)} %all-gather.3.cloned.1.call-done, bf16[4096,1024]{1,0:T(8,128)(2,1)} %all-gather.5.cloned.1.call-done, bf16[128,1024]{1,0:T(8,128)(2,1)} %param.10), kind=kOutput, calls=%fused_computation.13 | convolution fusion | flops 1074265984 | bytes 10224128 | tf_op jit(solution)/shard_map/dot_general | solution.py:24
  184.6 6.8 %psum.21 = f32[128]{0:T(128)S(1)} all-reduce(f32[128]{0:T(128)S(1)} %get-tuple-element.5), channel_id=1, replica_groups=mesh['groups'=2,'tok'=4,'mod'=2,'fsdp'=2] {'mod','fsdp'}, use_global_device_ids=true, to_apply=%region_1.2 | all-reduce | flops 128 | bytes 1024 | tf_op jit(solution)/shard_map/psum | solution.py:36
  191.5 0.1 fusion.7
  191.6 7.6 %all_gather.14 = bf16[128,2048]{1,0:T(8,128)(2,1)S(1)} all-gather(bf16[128,1024]{1,0:T(8,128)(2,1)S(1)} %fusion.7), channel_id=1, replica_groups=mesh['groups'=2,'tok'=4,'mod'=2,'fsdp'=2] {'mod'}, dimensions={1}, use_global_device_ids=true | all-gather | bytes 786432 | tf_op jit(solution)/shard_map/all_gather | solution.py:49
  199.1 0.2 convolution_convert_fusion.3
  199.4 14.7 %all_gather.15 = bf16[2,64,2048]{2,1,0:T(8,128)(2,1)S(1)} all-gather(bf16[2,16,2048]{2,1,0:T(8,128)(2,1)S(1)} %convolution_convert_fusion.3), channel_id=1, replica_groups=mesh['groups'=2,'tok'=4,'mod'=2,'fsdp'=2] {'tok'}, dimensions={1}, use_global_device_ids=true | all-gather | bytes 655360 | tf_op jit(solution)/shard_map/all_gather | solution.py:54
  214.1 11.3 %convolution_convert_fusion = bf16[2,64,2752]{2,1,0:T(8,128)(2,1)S(1)} fusion(bf16[2,64,2048]{2,1,0:T(8,128)(2,1)S(1)} %all_gather.15, bf16[2,2048,2752]{1,2,0:T(8,128)(2,1)} %param.18), kind=kOutput, calls=%fused_computation | convolution fusion | flops 1443192832 | bytes 23773184 | tf_op jit(solution)/shard_map/esd,edf->esf/dot_general | solution.py:56
  225.4 11.3 %convolution_convert_fusion.1 = bf16[2,64,2752]{2,1,0:T(8,128)(2,1)S(1)} fusion(bf16[2,64,2048]{2,1,0:T(8,128)(2,1)S(1)} %all_gather.15, bf16[2,2048,2752]{1,2,0:T(8,128)(2,1)} %param.17), kind=kOutput, calls=%fused_computation.1 | convolution fusion | flops 1443192832 | bytes 23773184 | tf_op jit(solution)/shard_map/esd,edf->esf/dot_general | solution.py:55
  236.7 1.4 pad_maximum_fusion
  238.1 0.0 all-reduce.2.cloned.1.call-update
  238.1 0.0 reduce-scatter.3.cloned.1.call-start
  238.2 19.4 %all-reduce.2.cloned.1.call-done = bf16[2,64,5504]{2,1,0:T(8,128)(2,1)} async-done(((bf16[2,64,5504]{2,1,0:T(8,128)(2,1)}), bf16[2,64,5504]{2,1,0:T(8,128)(2,1)}) %all-reduce.2.cloned.1.call-update) | async-done | bytes 1409040 | tf_op jit(solution)/shard_map/psum | solution.py:58
  257.6 1.5 convert_element_type.38
  259.1 12.3 %fusion.1 = bf16[64,2,2048]{2,0,1:T(8,128)(2,1)} fusion(bf16[2,2752,2048]{2,1,0:T(8,128)(2,1)} %param.19, f32[2,64,5504]{2,1,0:T(8,128)S(1)} %convert_element_type.38), kind=kOutput, calls=%fused_computation.5 | convolution fusion | flops 1445216256 | bytes 25952256 | tf_op jit(solution)/shard_map/esf,efd->sed/dot_general | solution.py:63
  271.4 0.0 reduce-scatter.3.cloned.1.call-update
  271.4 0.0 reduce-scatter.5.cloned.1.call-start
  271.5 0.0 copy-done
  271.5 0.4 fusion.6
  271.9 7.3 %psum.23 = f32[128,4]{0,1:T(4,128)S(1)} all-reduce(f32[128,4]{0,1:T(4,128)S(1)} %fusion.6), channel_id=1, replica_groups=mesh['groups'=2,'tok'=4,'mod'=2,'fsdp'=2] {'mod','fsdp'}, use_global_device_ids=true, to_apply=%region_4.5 | all-reduce | flops 512 | bytes 4096 | tf_op jit(solution)/shard_map/psum | solution.py:39
  279.2 0.2 fusion.13
  279.4 15.0 %reduce-scatter.3.cloned.1.call-done = bf16[16,2,2048]{2,0,1:T(8,128)(2,1)} async-done(((bf16[64,2,2048]{2,0,1:T(8,128)(2,1)}), bf16[16,2,2048]{2,0,1:T(8,128)(2,1)}) %reduce-scatter.3.cloned.1.call-update) | async-done | bytes 131088 | tf_op jit(solution)/shard_map/reduce_scatter | solution.py:62
  294.4 2.4 fusion
  296.8 0.0 reduce-scatter.5.cloned.1.call-update
  296.8 12.9 %reduce-scatter.5.cloned.1.call-done = bf16[128,1024]{1,0:T(8,128)(2,1)} async-done(((bf16[128,2048]{1,0:T(8,128)(2,1)}), bf16[128,1024]{1,0:T(8,128)(2,1)}) %reduce-scatter.5.cloned.1.call-update) | async-done | bytes 262160 | tf_op jit(solution)/shard_map/reduce_scatter | solution.py:75
  (4 shorter events, 0.0 us)
Async XLA Ops:
  6.5 264.9 %copy-start = (bf16[1024,4]{0,1:T(4,128)(2,1)S(1)}, bf16[1024,4]{0,1:T(4,128)(2,1)}, u32[]{:S(2)}) copy-start(bf16[1024,4]{0,1:T(4,128)(2,1)} %param.14) | copy-start | bytes 24580
  6.5 21.8 %all-gather.3.cloned.1.call-start = ((), (), s32[]{:S(2)}) async-start(), calls=%async_computation.2 | async-start | bytes 1310720 | tf_op jit(solution)/shard_map/all_gather | solution.py:22
  7.3 172.4 %all-gather.5.cloned.1.call-start = ((), (), s32[]{:S(2)}) async-start(), calls=%async_computation.3 | async-start | bytes 10485760 | tf_op jit(solution)/shard_map/all_gather | solution.py:26
  8.0 249.5 %all-reduce.2.cloned.1.call-start = ((), (), s32[]{:S(2)}) async-start(), calls=%async_computation.4 | async-start | bytes 2818048 | tf_op jit(solution)/shard_map/psum | solution.py:58
  238.1 56.3 %reduce-scatter.3.cloned.1.call-start = ((), (), s32[]{:S(2)}) async-start(), calls=%async_computation.5 | async-start | bytes 655360 | tf_op jit(solution)/shard_map/reduce_scatter | solution.py:62
  271.4 38.4 %reduce-scatter.5.cloned.1.call-start = ((), (), s32[]{:S(2)}) async-start(), calls=%async_computation.6 | async-start | bytes 786432 | tf_op jit(solution)/shard_map/reduce_scatter | solution.py:75
Sparse Core Ops, SparseCore 0:
  8.9 19.4 all-gather.2
  29.9 149.6 all-gather.4
  238.2 19.2 all-reduce.1
  271.5 22.8 reduce-scatter.2
  296.9 12.7 reduce-scatter.4
where the time goes:
time: 317 us; the launch traced here: 316 us
  waiting for transfers between devices  218 us (69%)
  matrix products  43.1 us (14%)
  blocking collectives  36.4 us (11%)
  between operations  13.8 us (4%)
  other arithmetic  3.74 us (1%)
    all_gather x1, waiting for transfers between devices, local(): lax.all_gather(out_proj, 'tok', axis=0, tiled=True)  151 us
    psum x1, waiting for transfers between devices, local(): lax.psum(partial_in.astype(jnp.bfloat16), 'fsdp').astype(jnp.float32)  19.4 us
    all_gather x1, waiting for transfers between devices, local(): full_context = lax.all_gather(context, ('mod', 'fsdp'), axis=1, tiled=True)  18.3 us
    reduce_scatter x1, waiting for transfers between devices, local(): lax.psum_scatter(jnp.einsum('esf,efd->sed', activation, down_weight, pref...  15 us
    all_gather x1, blocking collectives, local(): piece = lax.all_gather(chosen, 'tok', axis=1, tiled=True)  14.7 us
    reduce_scatter x1, waiting for transfers between devices, local(): lax.psum_scatter(mixed_rows.astype(jnp.bfloat16), 'mod', scatter_dimensio...  12.9 us
    dot_general x1, matrix products, local(): jnp.einsum('esf,efd->sed', activation, down_weight, preferred_element_typ...  12.3 us
    dot_general x1, matrix products, local(): jnp.einsum('esd,edf->esf', piece, gate_weight, preferred_element_type=jnp...  11.3 us
  transfers between devices with their start and end apart: 5, of which 5 were waited for; matrix products, arithmetic and copies ran while one was open for 1% of the time, Pallas kernels for 0%

commit v1 on v0

--- a/solution.py
+++ b/solution.py
@@ -5,6 +5,17 @@
 
 D = 4096
 BLOCK = 128
+
+
+def take_rows_for(x_in, along_dim):
+    x_in = jnp.moveaxis(x_in, 0, along_dim)
+    value_now = x_in.shape
+    side_arr = x_in.reshape(
+        *value_now[:along_dim],
+        value_now[along_dim] * value_now[along_dim + 1],
+        *value_now[along_dim + 2 :]
+    )
+    return side_arr
 
 
 def local(
@@ -51,7 +62,21 @@
         "ecr,rd->ecd", own_pick, half_rows, preferred_element_type=jnp.float32
     ).astype(jnp.bfloat16)
     unit_count = gate_weight.shape[2]
-    piece = lax.all_gather(chosen, "tok", axis=1, tiled=True)
+    count_all = lax.axis_size("tok")
+    column = [(w, (w + 1) % count_all) for w in range(count_all)]
+    heap = [(idx, k) for k, idx in column]
+    arr_next, next_value = ([], [])
+    j = 0
+    while j < count_all - 1:
+        if j % 2 == 0:
+            arr_next.append(lax.ppermute(arr_next[-1] if arr_next else chosen, "tok", column))
+        else:
+            next_value.append(lax.ppermute(next_value[-1] if next_value else chosen, "tok", heap))
+        j = j + 1
+    w_next = jnp.stack([*arr_next[::-1], chosen, *next_value], axis=0)
+    top = lax.axis_index("tok") - len(arr_next)
+    w_next = w_next[(jnp.arange(count_all) - top) % count_all]
+    piece = take_rows_for(w_next, 1)
     gate_part = jnp.einsum("esd,edf->esf", piece, gate_weight, preferred_element_type=jnp.float32)
     up_part = jnp.einsum("esd,edf->esf", piece, up_weight, preferred_element_type=jnp.float32)
     partial_in = jnp.concatenate((gate_part, up_part), axis=2)

time: 317 us -> 316 us (level)
  blocking collectives: 36.4 us -> 21.7 us
  waiting for transfers between devices: 218 us -> 228 us
  starting transfers between devices: 0.16 us -> 4.03 us
    all_gather x1 -> x0, blocking collectives: 14.7 us -> none  [local(): piece = lax.all_gather(chosen, 'tok', axis=1, tiled=True)]
    ppermute x0 -> x3, waiting for transfers between devices: none -> 9.77 us  [the longest x2 9.77 us: local(): lax.ppermute(arr_next[-1] if arr_next else chosen, 'tok', column)]
    ppermute x0 -> x3, starting transfers between devices: none -> 3.87 us  [the longest x1 3.81 us: local(): lax.ppermute(next_value[-1] if next_value else chosen, 'tok', heap)]
  transfers between devices with their start and end apart: 5 -> 8, of which waited for: 5 -> 7; matrix products, arithmetic and copies ran while one was open for 1% -> 1% of each run, Pallas kernels for 0% -> 0%
where the time goes in v1:
time: 316 us; the launch traced here: 315 us
  waiting for transfers between devices  228 us (72%)
  matrix products  43.1 us (14%)
  blocking collectives  21.7 us (7%)
  between operations  13.9 us (4%)
  starting transfers between devices  4.03 us (1%)
  other arithmetic  3.81 us (1%)
    all_gather x1, waiting for transfers between devices, local(): lax.all_gather(out_proj, 'tok', axis=0, tiled=True)  151 us
    psum x1, waiting for transfers between devices, local(): lax.psum(partial_in.astype(jnp.bfloat16), 'fsdp').astype(jnp.float32)  18.9 us
    all_gather x1, waiting for transfers between devices, local(): full_context = lax.all_gather(context, ('mod', 'fsdp'), axis=1, tiled=True)  18.3 us
    reduce_scatter x1, waiting for transfers between devices, local(): lax.psum_scatter(jnp.einsum('esf,efd->sed', activation, down_weight, pref...  15 us
    reduce_scatter x1, waiting for transfers between devices, local(): lax.psum_scatter(mixed_rows.astype(jnp.bfloat16), 'mod', scatter_dimensio...  12.9 us
    dot_general x1, matrix products, local(): jnp.einsum('esf,efd->sed', activation, down_weight, preferred_element_typ...  12.3 us
    dot_general x1, matrix products, local(): jnp.einsum('esd,edf->esf', piece, gate_weight, preferred_element_type=jnp...  11.3 us
    dot_general x1, matrix products, local(): jnp.einsum('esd,edf->esf', piece, up_weight, preferred_element_type=jnp.f...  11.3 us
  transfers between devices with their start and end apart: 8, of which 7 were waited for; matrix products, arithmetic and copies ran while one was open for 1% of the time, Pallas kernels for 0%

profile of v1, /device:TPU:0, one launch (start us, length us, event | category | flops | bytes accessed | tf_op | source)
XLA Modules:
  0.0 315.4 jit_solution(17556617156485565791)
XLA Ops:
  6.5 0.0 copy-start
  6.5 0.0 all-gather.3.cloned.1.call-start
  6.5 0.7 all-gather.3.cloned.1.call-update
  7.3 0.0 all-gather.5.cloned.1.call-start
  7.3 0.7 all-gather.5.cloned.1.call-update
  8.0 0.0 all-reduce.2.cloned.1.call-start
  8.7 0.7 convert_element_type.35
  9.4 0.7 constant_dynamic-slice_fusion.1
  10.1 18.3 %all-gather.3.cloned.1.call-done = bf16[128,4096]{1,0:T(8,128)(2,1)} async-done(((bf16[128,1024]{1,0:T(8,128)(2,1)}), bf16[128,4096]{1,0:T(8,128)(2,1)}) %all-gather.3.cloned.1.call-update) | async-done | bytes 1048592 | tf_op jit(solution)/shard_map/all_gather | solution.py:33
  28.4 151.2 %all-gather.5.cloned.1.call-done = bf16[4096,1024]{1,0:T(8,128)(2,1)} async-done(((bf16[1024,1024]{1,0:T(8,128)(2,1)}), bf16[4096,1024]{1,0:T(8,128)(2,1)}) %all-gather.5.cloned.1.call-update) | async-done | bytes 8388624 | tf_op jit(solution)/shard_map/all_gather | solution.py:37
  179.6 5.0 %multiply_reduce_fusion = (f32[128]{0:T(128)S(1)}, f32[128,1024]{1,0:T(8,128)S(1)}) fusion(bf16[128,4096]{1,0:T(8,128)(2,1)} %all-gather.3.cloned.1.call-done, bf16[4096,1024]{1,0:T(8,128)(2,1)} %all-gather.5.cloned.1.call-done, bf16[128,1024]{1,0:T(8,128)(2,1)} %param.10), kind=kOutput, calls=%fused_computation.15 | convolution fusion | flops 1074265984 | bytes 10224128 | tf_op jit(solution)/shard_map/dot_general | solution.py:35
  184.6 6.8 %psum.21 = f32[128]{0:T(128)S(1)} all-reduce(f32[128]{0:T(128)S(1)} %get-tuple-element.5), channel_id=1, replica_groups=mesh['groups'=2,'tok'=4,'mod'=2,'fsdp'=2] {'mod','fsdp'}, use_global_device_ids=true, to_apply=%region_1.2 | all-reduce | flops 128 | bytes 1024 | tf_op jit(solution)/shard_map/psum | solution.py:47
  191.5 0.1 fusion.7
  191.6 7.6 %all_gather.11 = bf16[128,2048]{1,0:T(8,128)(2,1)S(1)} all-gather(bf16[128,1024]{1,0:T(8,128)(2,1)S(1)} %fusion.7), channel_id=1, replica_groups=mesh['groups'=2,'tok'=4,'mod'=2,'fsdp'=2] {'mod'}, dimensions={1}, use_global_device_ids=true | all-gather | bytes 786432 | tf_op jit(solution)/shard_map/all_gather | solution.py:60
  199.1 0.2 convolution_convert_fusion.3
  199.4 0.1 collective-permute-start
  199.5 3.8 %collective-permute-start.2 = (bf16[2,16,2048]{2,1,0:T(8,128)(2,1)S(1)}, bf16[2,16,2048]{2,1,0:T(8,128)(2,1)S(1)}, u32[]{:S(2)}, u32[]{:S(2)}) collective-permute-start(bf16[2,16,2048]{2,1,0:T(8,128)(2,1)S(1)} %convolution_convert_fusion.3), channel_id=1, source_target_pairs={{4,0},{8,4},{12,8},{0,12},{5,1},{9,5},{13,9},{1,13},{6,2},{10,6},{... | collective-permute-start | bytes 393224 | tf_op jit(solution)/shard_map/ppermute | solution.py:74
  203.3 3.0 collective-permute-done
  206.3 0.0 collective-permute-start.1
  206.3 0.0 collective-permute-done.2
  206.4 6.7 %collective-permute-done.1 = bf16[2,16,2048]{2,1,0:T(8,128)(2,1)S(1)} collective-permute-done((bf16[2,16,2048]{2,1,0:T(8,128)(2,1)S(1)}, bf16[2,16,2048]{2,1,0:T(8,128)(2,1)S(1)}, u32[]{:S(2)}, u32[]{:S(2)}) %collective-permute-start.1) | collective-permute-done | bytes 131104 | tf_op jit(solution)/shard_map/ppermute | solution.py:72
  213.1 0.1 pad_maximum_fusion.1
  213.1 0.6 gather_fusion
  213.8 11.3 %convolution_convert_fusion = bf16[2,64,2752]{2,1,0:T(8,128)(2,1)S(1)} fusion(bf16[2,64,2048]{2,1,0:T(8,128)(2,1)S(1)} %bitcast.35, bf16[2,2048,2752]{1,2,0:T(8,128)(2,1)} %param.18), kind=kOutput, calls=%fused_computation.1 | convolution fusion | flops 1443192832 | bytes 23773184 | tf_op jit(solution)/shard_map/esd,edf->esf/dot_general | solution.py:81
  225.1 11.3 %convolution_convert_fusion.1 = bf16[2,64,2752]{2,1,0:T(8,128)(2,1)S(1)} fusion(bf16[2,64,2048]{2,1,0:T(8,128)(2,1)S(1)} %bitcast.36, bf16[2,2048,2752]{1,2,0:T(8,128)(2,1)} %param.17), kind=kOutput, calls=%fused_computation.2 | convolution fusion | flops 1443192832 | bytes 23773184 | tf_op jit(solution)/shard_map/esd,edf->esf/dot_general | solution.py:80
  236.4 1.4 pad_maximum_fusion
  237.8 0.0 all-reduce.2.cloned.1.call-update
  237.8 0.0 reduce-scatter.3.cloned.1.call-start
  237.8 18.9 %all-reduce.2.cloned.1.call-done = bf16[2,64,5504]{2,1,0:T(8,128)(2,1)} async-done(((bf16[2,64,5504]{2,1,0:T(8,128)(2,1)}), bf16[2,64,5504]{2,1,0:T(8,128)(2,1)}) %all-reduce.2.cloned.1.call-update) | async-done | bytes 1409040 | tf_op jit(solution)/shard_map/psum | solution.py:83
  256.7 1.5 convert_element_type.38
  258.2 12.3 %fusion.1 = bf16[64,2,2048]{2,0,1:T(8,128)(2,1)} fusion(bf16[2,2752,2048]{2,1,0:T(8,128)(2,1)} %param.19, f32[2,64,5504]{2,1,0:T(8,128)S(1)} %convert_element_type.38), kind=kOutput, calls=%fused_computation.6 | convolution fusion | flops 1445216256 | bytes 25952256 | tf_op jit(solution)/shard_map/esf,efd->sed/dot_general | solution.py:88
  270.5 0.0 reduce-scatter.3.cloned.1.call-update
  270.6 0.0 reduce-scatter.5.cloned.1.call-start
  270.6 0.0 copy-done
  270.6 0.4 fusion.6
  271.0 7.3 %psum.23 = f32[128,4]{0,1:T(4,128)S(1)} all-reduce(f32[128,4]{0,1:T(4,128)S(1)} %fusion.6), channel_id=1, replica_groups=mesh['groups'=2,'tok'=4,'mod'=2,'fsdp'=2] {'mod','fsdp'}, use_global_device_ids=true, to_apply=%region_4.5 | all-reduce | flops 512 | bytes 4096 | tf_op jit(solution)/shard_map/psum | solution.py:50
  278.3 0.2 fusion.13
  278.5 15.0 %reduce-scatter.3.cloned.1.call-done = bf16[16,2,2048]{2,0,1:T(8,128)(2,1)} async-done(((bf16[64,2,2048]{2,0,1:T(8,128)(2,1)}), bf16[16,2,2048]{2,0,1:T(8,128)(2,1)}) %reduce-scatter.3.cloned.1.call-update) | async-done | bytes 131088 | tf_op jit(solution)/shard_map/reduce_scatter | solution.py:87
  293.5 2.4 fusion
  295.9 0.0 reduce-scatter.5.cloned.1.call-update
  296.0 12.9 %reduce-scatter.5.cloned.1.call-done = bf16[128,1024]{1,0:T(8,128)(2,1)} async-done(((bf16[128,2048]{1,0:T(8,128)(2,1)}), bf16[128,1024]{1,0:T(8,128)(2,1)}) %reduce-scatter.5.cloned.1.call-update) | async-done | bytes 262160 | tf_op jit(solution)/shard_map/reduce_scatter | solution.py:100
  (7 shorter events, 0.1 us)
Async XLA Ops:
  6.5 264.1 %copy-start = (bf16[1024,4]{0,1:T(4,128)(2,1)S(1)}, bf16[1024,4]{0,1:T(4,128)(2,1)}, u32[]{:S(2)}) copy-start(bf16[1024,4]{0,1:T(4,128)(2,1)} %param.14) | copy-start | bytes 24580
  6.5 21.8 %all-gather.3.cloned.1.call-start = ((), (), s32[]{:S(2)}) async-start(), calls=%async_computation.2 | async-start | bytes 1310720 | tf_op jit(solution)/shard_map/all_gather | solution.py:33
  7.3 172.4 %all-gather.5.cloned.1.call-start = ((), (), s32[]{:S(2)}) async-start(), calls=%async_computation.3 | async-start | bytes 10485760 | tf_op jit(solution)/shard_map/all_gather | solution.py:37
  8.0 248.7 %all-reduce.2.cloned.1.call-start = ((), (), s32[]{:S(2)}) async-start(), calls=%async_computation.4 | async-start | bytes 2818048 | tf_op jit(solution)/shard_map/psum | solution.py:83
  199.4 6.9 %collective-permute-start = (bf16[2,16,2048]{2,1,0:T(8,128)(2,1)S(1)}, bf16[2,16,2048]{2,1,0:T(8,128)(2,1)S(1)}, u32[]{:S(2)}, u32[]{:S(2)}) collective-permute-start(bf16[2,16,2048]{2,1,0:T(8,128)(2,1)S(1)} %convolution_convert_fusion.3), channel_id=1, source_target_pairs={{0,4},{4,8},{8,12},{12,0},{1,5},{5,9},{9,13},{13,1},{2,6},{6,10},{... | collective-permute-start | bytes 393224 | tf_op jit(solution)/shard_map/ppermute | solution.py:72
  199.5 6.9 %collective-permute-start.2 = (bf16[2,16,2048]{2,1,0:T(8,128)(2,1)S(1)}, bf16[2,16,2048]{2,1,0:T(8,128)(2,1)S(1)}, u32[]{:S(2)}, u32[]{:S(2)}) collective-permute-start(bf16[2,16,2048]{2,1,0:T(8,128)(2,1)S(1)} %convolution_convert_fusion.3), channel_id=1, source_target_pairs={{4,0},{8,4},{12,8},{0,12},{5,1},{9,5},{13,9},{1,13},{6,2},{10,6},{... | collective-permute-start | bytes 393224 | tf_op jit(solution)/shard_map/ppermute | solution.py:74
  206.3 6.8 %collective-permute-start.1 = (bf16[2,16,2048]{2,1,0:T(8,128)(2,1)S(1)}, bf16[2,16,2048]{2,1,0:T(8,128)(2,1)S(1)}, u32[]{:S(2)}, u32[]{:S(2)}) collective-permute-start(bf16[2,16,2048]{2,1,0:T(8,128)(2,1)S(1)} %collective-permute-done), channel_id=1, source_target_pairs={{0,4},{4,8},{8,12},{12,0},{1,5},{5,9},{9,13},{13,1},{2,6},{6,10},{... | collective-permute-start | bytes 393224 | tf_op jit(solution)/shard_map/ppermute | solution.py:72
  237.8 55.7 %reduce-scatter.3.cloned.1.call-start = ((), (), s32[]{:S(2)}) async-start(), calls=%async_computation.5 | async-start | bytes 655360 | tf_op jit(solution)/shard_map/reduce_scatter | solution.py:87
  270.6 38.3 %reduce-scatter.5.cloned.1.call-start = ((), (), s32[]{:S(2)}) async-start(), calls=%async_computation.6 | async-start | bytes 786432 | tf_op jit(solution)/shard_map/reduce_scatter | solution.py:100
Sparse Core Ops, SparseCore 0:
  8.9 19.4 all-gather.2
  29.9 149.6 all-gather.4
  237.9 18.7 all-reduce.1
  270.7 22.8 reduce-scatter.2
  296.1 12.7 reduce-scatter.4
